TPU v7x, 512 devices: a whole 4x8x8 slice. The times are simulated.
512 devices in a mesh: mp: 2 (over z_lo), blk: 32 (over x, y), tok: 8 (over z_hi, core).
Axes of the slice: x: 4, y: 8, z: 8 (z_hi: 4, z_lo: 2; z = z_hi * 2 + z_lo), core: 2. Of those that a mesh axis runs over, the one named last changes fastest.
Arguments:
- inputs: bfloat16 [2, 1024, 28672], P('mp', 'tok', 'blk'), may hold values from -1.1953125 to 1.1953125
- down_weight: bfloat16 [2, 512, 28672], P('mp', None, 'blk'), may hold values from -0.03125 to 0.03125
Outputs:
- denominator: float32 [1024, 28672], P('blk', 'tok')
- numerator: float32 [1024, 512], P('blk', 'tok')
All inputs are finite; a program needn't handle non-finite values.
Results may differ from a plain program's by a relative error of at most 0.0003.
Values may be sent and summed in bfloat16 or wider, within the bound.
No kernel may reach another device: no remote copies, remote signals or barrier semaphores. Data moves between devices by JAX's collectives and lax.ppermute only.
A program may use at most 64 MiB of HBM per device.

v0:
```python
import jax
import jax.numpy as jnp
from jax import lax
from jax.sharding import PartitionSpec as P

DIN = 28672
COLS = 512
ROW_DEV = 32
OFF_SCALE = 0.9


def local(inputs, down_weight):
    x_local = inputs[0]
    w_local = down_weight[0]
    span_width = x_local.shape[1]
    x_rows = x_local[:, :ROW_DEV]
    blk_index = lax.axis_index("blk")
    tok_index = lax.axis_index("tok")
    tok_count = lax.axis_size("tok")
    col_share = DIN // tok_count
    col_parts = COLS // tok_count
    partial_value = lax.dot_general(
        x_rows,
        lax.all_gather(x_local, "blk", axis=1, tiled=True),
        (((0,), (0,)), ((), ())),
        preferred_element_type=jnp.float32,
    )
    gram_panel = lax.psum(partial_value, "tok")
    col_ids = lax.broadcasted_iota(jnp.int32, gram_panel.shape, 1)
    row_ids = lax.broadcasted_iota(jnp.int32, gram_panel.shape, 0)
    on_diag = col_ids == blk_index * span_width + row_ids
    reduced = jnp.where(on_diag, gram_panel, OFF_SCALE * gram_panel)
    denominator = lax.dynamic_slice_in_dim(reduced, tok_index * col_share, col_share, 1)
    w_group = lax.dynamic_slice_in_dim(w_local, tok_index * col_parts, col_parts, 0)
    numerator = lax.dot_general(
        reduced,
        lax.all_gather(w_group, "blk", axis=1, tiled=True).astype(jnp.float32),
        (((1,), (1,)), ((), ())),
        precision=lax.Precision.HIGHEST,
        preferred_element_type=jnp.float32,
    )
    denominator, numerator = lax.psum((denominator, numerator), "mp")
    return (denominator, numerator)


def solution(mesh):
    placed = (P("mp", "tok", "blk"), P("mp", None, "blk"))
    return jax.shard_map(
        local,
        mesh=mesh,
        in_specs=placed,
        out_specs=(P("blk", "tok"), P("blk", "tok")),
        check_vma=False,
    )
```

profile of v0, /device:TPU:1, one launch (start us, length us, event | category | flops | bytes accessed | tf_op | source)
XLA Modules:
  0.0 373.1 jit_solution(2469359406197091980)
XLA Ops:
  7.2 0.0 copy-start
  7.2 0.0 all-gather.5.cloned.1.call-start
  7.2 0.7 all-gather.5.cloned.1.call-update
  7.9 0.0 all-reduce.3.cloned.1.call-start
  8.0 106.5 %all-gather.5.cloned.1.call-done = bf16[1,128,28672]{2,1,0:T(8,128)(2,1)} async-done(((bf16[1,128,896]{2,1,0:T(8,128)(2,1)}), bf16[1,128,28672]{2,1,0:T(8,128)(2,1)}) %all-gather.5.cloned.1.call-update) | async-done | bytes 7340048 | tf_op jit(solution)/shard_map/all_gather | solution.py:24
  114.4 6.1 %fusion = f32[32,28672]{1,0:T(8,128)} fusion(bf16[1,128,28672]{2,1,0:T(8,128)(2,1)} %all-gather.5.cloned.1.call-done, bf16[128,896]{1,0:T(8,128)(2,1)} %bitcast.8), kind=kOutput, calls=%fused_computation | convolution fusion | flops 234881024 | bytes 11042816 | tf_op jit(solution)/shard_map/dot_general | solution.py:22
  120.6 0.0 all-reduce.3.cloned.1.call-update
  120.6 0.0 all-gather.7.cloned.1.call-start
  120.7 0.0 copy-done
  120.7 0.7 constant_dynamic-slice_fusion
  121.3 0.0 all-gather.7.cloned.1.call-update
  121.4 0.0 all-reduce.5.cloned.1.call-start
  121.4 107.3 %all-reduce.3.cloned.1.call-done = f32[32,28672]{1,0:T(8,128)} async-done(((f32[32,28672]{1,0:T(8,128)}), f32[32,28672]{1,0:T(8,128)}) %all-reduce.3.cloned.1.call-update) | async-done | bytes 3670032 | tf_op jit(solution)/shard_map/psum | solution.py:28
  228.8 2.5 multiply_select_fusion
  231.3 0.0 copy-start.1
  231.3 1.8 copy-done.1
  233.1 0.8 constant_dynamic-slice_fusion.1
  233.9 0.0 all-reduce.5.cloned.1.call-update
  234.0 82.6 %all-gather.7.cloned.1.call-done = bf16[1,64,28672]{2,1,0:T(8,128)(2,1)} async-done(((bf16[1,64,896]{2,1,0:T(8,128)(2,1)}), bf16[1,64,28672]{2,1,0:T(8,128)(2,1)}) %all-gather.7.cloned.1.call-update) | async-done | bytes 3670032 | tf_op jit(solution)/shard_map/all_gather | solution.py:37
  316.6 6.1 %fusion.2 = f32[32,64]{1,0:T(8,128)S(1)} fusion(f32[32,28672]{1,0:T(8,128)} %copy-done.1, bf16[1,64,28672]{2,1,0:T(8,128)(2,1)} %all-gather.7.cloned.1.call-done), kind=kOutput, calls=%fused_computation.3 | convolution fusion | flops 704643072 | bytes 7348224 | tf_op jit(solution)/shard_map/dot_general | solution.py:35
  322.7 6.9 %psum.23 = f32[32,64]{1,0:T(8,128)} all-reduce(f32[32,64]{1,0:T(8,128)S(1)} %fusion.2), channel_id=1, replica_groups=mesh['mp'=2,'blk'=32,'tok'=8] {'mp'}, use_global_device_ids=true, to_apply=%region_2.3 | all-reduce | flops 2048 | bytes 16384 | tf_op jit(solution)/shard_map/psum | solution.py:42
  329.6 35.2 %all-reduce.5.cloned.1.call-done = f32[32,3584]{1,0:T(8,128)} async-done(((f32[32,3584]{1,0:T(8,128)}), f32[32,3584]{1,0:T(8,128)}) %all-reduce.5.cloned.1.call-update) | async-done | bytes 458768 | tf_op jit(solution)/shard_map/psum | solution.py:42
  364.8 1.8 copy.6
  (1 shorter events, 0.0 us)
Async XLA Ops:
  7.2 113.5 %copy-start = (bf16[1,512,896]{2,1,0:T(8,128)(2,1)S(1)}, bf16[1,512,896]{2,1,0:T(8,128)(2,1)}, u32[]{:S(2)}) copy-start(bf16[1,512,896]{2,1,0:T(8,128)(2,1)} %param.3) | copy-start | bytes 2752516
  7.2 107.3 %all-gather.5.cloned.1.call-start = ((), (), s32[]{:S(2)}) async-start(), calls=%async_computation.2 | async-start | bytes 7569408 | tf_op jit(solution)/shard_map/all_gather | solution.py:24
  7.9 220.9 %all-reduce.3.cloned.1.call-start = ((), (), s32[]{:S(2)}) async-start(), calls=%async_computation | async-start | bytes 7340032 | tf_op jit(solution)/shard_map/psum | solution.py:28
  120.6 196.0 %all-gather.7.cloned.1.call-start = ((), (), s32[]{:S(2)}) async-start(), calls=%async_computation.3 | async-start | bytes 3784704 | tf_op jit(solution)/shard_map/all_gather | solution.py:37
  121.4 243.4 %all-reduce.5.cloned.1.call-start = ((), (), s32[]{:S(2)}) async-start(), calls=%async_computation.1 | async-start | bytes 917504 | tf_op jit(solution)/shard_map/psum | solution.py:42
  231.3 1.8 copy-start.1
Sparse Core Ops, SparseCore 0:
  11.2 103.2 all-gather.4
  120.7 107.9 all-reduce.2
  232.0 84.5 all-gather.6
  319.9 44.7 all-reduce.4
where the time goes:
time: 373 us
  waiting for transfers between devices  332 us (89%)
  between operations  13.8 us (4%)
  matrix products  12.3 us (3%)
  blocking collectives  6.89 us (2%)
  local copies, waits for them, and re-layouts  5.12 us (1%)
    psum x1, waiting for transfers between devices, local(): gram_panel = lax.psum(partial_value, 'tok')  107 us
    all_gather x1, waiting for transfers between devices, local(): lax.all_gather(x_local, 'blk', axis=1, tiled=True)  106 us
    all_gather x1, waiting for transfers between devices, local(): lax.all_gather(w_group, 'blk', axis=1, tiled=True).astype(jnp.float32)  82.6 us
    psum x1, waiting for transfers between devices, local(): denominator, numerator = lax.psum((denominator, numerator), 'mp')  35.2 us
  transfers between devices with their start and end apart: 4, of which 4 were waited for; matrix products, arithmetic and copies ran while one was open for 3% of the time, Pallas kernels for 0%

commit v1 on v0

--- a/solution.py
+++ b/solution.py
@@ -34,7 +34,9 @@
     w_group = lax.dynamic_slice_in_dim(w_local, tok_index * col_parts, col_parts, 0)
     numerator = lax.dot_general(
         reduced,
-        lax.all_gather(w_group, "blk", axis=1, tiled=True).astype(jnp.float32),
+        jnp.concatenate(
+            lax.all_to_all(jnp.stack([w_group] * lax.axis_size("blk")), "blk", 0, 0), axis=1
+        ).astype(jnp.float32),
         (((1,), (1,)), ((), ())),
         precision=lax.Precision.HIGHEST,
         preferred_element_type=jnp.float32,

time: 373 us -> 288 us (0.77)
  waiting for transfers between devices: 332 us -> 237 us
  starting transfers between devices: 0.16 us -> 6.2 us
  local copies, waits for them, and re-layouts: 5.12 us -> 10 us
    all_gather x1 -> x0, waiting for transfers between devices: 82.6 us -> none  [local(): lax.all_gather(w_group, 'blk', axis=1, tiled=True).astype(jnp.float32)]
    psum x1, waiting for transfers between devices: 107 us -> 99.4 us  [local(): gram_panel = lax.psum(partial_value, 'tok')]
    all_to_all x0 -> x1, starting transfers between devices: none -> 6.09 us  [local(): lax.all_to_all(jnp.stack([w_group] * lax.axis_size('blk')), 'blk', 0, 0)]
    psum x1, waiting for transfers between devices: 35.2 us -> 30.9 us  [local(): denominator, numerator = lax.psum((denominator, numerator), 'mp')]
  transfers between devices with their start and end apart: 4 -> 4, of which waited for: 4 -> 3; matrix products, arithmetic and copies ran while one was open for 3% -> 4% of each run, Pallas kernels for 0% -> 0%
where the time goes in v1:
time: 288 us
  waiting for transfers between devices  237 us (82%)
  between operations  13.8 us (5%)
  local copies, waits for them, and re-layouts  10 us (3%)
  matrix products  9.11 us (3%)
  blocking collectives  8.58 us (3%)
  starting transfers between devices  6.2 us (2%)
    all_gather x1, waiting for transfers between devices, local(): lax.all_gather(x_local, 'blk', axis=1, tiled=True)  106 us
    psum x1, waiting for transfers between devices, local(): gram_panel = lax.psum(partial_value, 'tok')  99.4 us
    psum x1, waiting for transfers between devices, local(): denominator, numerator = lax.psum((denominator, numerator), 'mp')  30.9 us
    psum x1, blocking collectives, local(): denominator, numerator = lax.psum((denominator, numerator), 'mp')  8.58 us
    dot_general x1, matrix products, local(): lax.dot_general(x_rows, lax.all_gather(x_local, 'blk', axis=1, tiled=True...  6.14 us
    all_to_all x1, starting transfers between devices, local(): lax.all_to_all(jnp.stack([w_group] * lax.axis_size('blk')), 'blk', 0, 0)  6.09 us
  transfers between devices with their start and end apart: 4, of which 3 were waited for; matrix products, arithmetic and copies ran while one was open for 4% of the time, Pallas kernels for 0%

profile of v1, /device:TPU:1, one launch (start us, length us, event | category | flops | bytes accessed | tf_op | source)
XLA Modules:
  0.0 287.7 jit_solution(10449956251542789773)
XLA Ops:
  7.2 0.0 copy-start
  7.2 0.0 all-gather.3.cloned.1.call-start
  7.2 0.7 all-gather.3.cloned.1.call-update
  7.9 0.0 all-reduce.3.cloned.1.call-start
  8.0 106.5 %all-gather.3.cloned.1.call-done = bf16[1,128,28672]{2,1,0:T(8,128)(2,1)} async-done(((bf16[1,128,896]{2,1,0:T(8,128)(2,1)}), bf16[1,128,28672]{2,1,0:T(8,128)(2,1)}) %all-gather.3.cloned.1.call-update) | async-done | bytes 7340048 | tf_op jit(solution)/shard_map/all_gather | solution.py:24
  114.4 6.1 %fusion = f32[32,28672]{1,0:T(8,128)} fusion(bf16[1,128,28672]{2,1,0:T(8,128)(2,1)} %all-gather.3.cloned.1.call-done, bf16[128,896]{1,0:T(8,128)(2,1)} %bitcast.12), kind=kOutput, calls=%fused_computation | convolution fusion | flops 234881024 | bytes 11042816 | tf_op jit(solution)/shard_map/dot_general | solution.py:22
  120.6 0.0 all-reduce.3.cloned.1.call-update
  120.6 0.0 copy-done
  120.7 2.4 stack.5
  123.0 6.1 %all-to-all-start = ((bf16[32,64,896]{2,1,0:T(8,128)(2,1)}), bf16[32,64,896]{2,1,0:T(8,128)(2,1)}, u32[]{:S(2)}, u32[]{:S(2)}) async-start(bf16[32,64,896]{2,1,0:T(8,128)(2,1)} %stack.5), calls=%async_computation | async-start | bytes 7340032 | tf_op jit(solution)/shard_map/all_to_all | solution.py:38
  129.1 0.0 all-reduce.5.cloned.1.call-start
  129.2 99.4 %all-reduce.3.cloned.1.call-done = f32[32,28672]{1,0:T(8,128)} async-done(((f32[32,28672]{1,0:T(8,128)}), f32[32,28672]{1,0:T(8,128)}) %all-reduce.3.cloned.1.call-update) | async-done | bytes 3670032 | tf_op jit(solution)/shard_map/psum | solution.py:28
  228.5 2.5 multiply_select_fusion
  231.1 0.0 copy-start.1
  231.1 1.9 copy-done.1
  233.0 0.8 constant_dynamic-slice_fusion
  233.8 0.0 all-reduce.5.cloned.1.call-update
  233.8 0.0 all-to-all-done
  233.8 2.7 copy.5
  236.5 0.4 copy-done.2
  237.0 3.0 %fusion.3 = f32[32,64]{1,0:T(8,128)S(1)} fusion(f32[32,28672]{1,0:T(8,128)S(1)} %copy-done.2, bf16[64,28672]{1,0:T(8,128)(2,1)S(1)} %bitcast.11), kind=kOutput, calls=%fused_computation.8 | convolution fusion | flops 704643072 | bytes 7348224 | tf_op jit(solution)/shard_map/dot_general | solution.py:35
  239.9 8.6 %psum.23 = f32[32,64]{1,0:T(8,128)} all-reduce(f32[32,64]{1,0:T(8,128)S(1)} %fusion.3), channel_id=1, replica_groups=mesh['mp'=2,'blk'=32,'tok'=8] {'mp'}, use_global_device_ids=true, to_apply=%region_2.3 | all-reduce | flops 2048 | bytes 16384 | tf_op jit(solution)/shard_map/psum | solution.py:44
  248.5 30.9 %all-reduce.5.cloned.1.call-done = f32[32,3584]{1,0:T(8,128)} async-done(((f32[32,3584]{1,0:T(8,128)}), f32[32,3584]{1,0:T(8,128)}) %all-reduce.5.cloned.1.call-update) | async-done | bytes 458768 | tf_op jit(solution)/shard_map/psum | solution.py:44
  279.4 1.8 copy.8
  (3 shorter events, 0.0 us)
Async XLA Ops:
  7.2 113.5 %copy-start = (bf16[1,512,896]{2,1,0:T(8,128)(2,1)S(1)}, bf16[1,512,896]{2,1,0:T(8,128)(2,1)}, u32[]{:S(2)}) copy-start(bf16[1,512,896]{2,1,0:T(8,128)(2,1)} %param.3) | copy-start | bytes 2752516
  7.2 107.3 %all-gather.3.cloned.1.call-start = ((), (), s32[]{:S(2)}) async-start(), calls=%async_computation.3 | async-start | bytes 7569408 | tf_op jit(solution)/shard_map/all_gather | solution.py:24
  7.9 220.6 %all-reduce.3.cloned.1.call-start = ((), (), s32[]{:S(2)}) async-start(), calls=%async_computation.1 | async-start | bytes 7340032 | tf_op jit(solution)/shard_map/psum | solution.py:28
  123.0 110.8 %all-to-all-start = ((bf16[32,64,896]{2,1,0:T(8,128)(2,1)}), bf16[32,64,896]{2,1,0:T(8,128)(2,1)}, u32[]{:S(2)}, u32[]{:S(2)}) async-start(bf16[32,64,896]{2,1,0:T(8,128)(2,1)} %stack.5), calls=%async_computation | async-start | bytes 7340032 | tf_op jit(solution)/shard_map/all_to_all | solution.py:38
  129.1 150.3 %all-reduce.5.cloned.1.call-start = ((), (), s32[]{:S(2)}) async-start(), calls=%async_computation.2 | async-start | bytes 917504 | tf_op jit(solution)/shard_map/psum | solution.py:44
  231.1 1.9 copy-start.1
  233.8 3.1 %copy-start.2 = (f32[32,28672]{1,0:T(8,128)S(1)}, f32[32,28672]{1,0:T(8,128)}, u32[]{:S(2)}) copy-start(f32[32,28672]{1,0:T(8,128)} %copy-done.1) | copy-start | bytes 11010052
Sparse Core Ops, SparseCore 0:
  11.2 103.2 all-gather.2
  120.7 107.7 all-reduce.2
  233.9 45.4 all-reduce.4

commit v2 on v0

--- a/solution.py
+++ b/solution.py
@@ -25,7 +25,7 @@
         (((0,), (0,)), ((), ())),
         preferred_element_type=jnp.float32,
     )
-    gram_panel = lax.psum(partial_value, "tok")
+    gram_panel = jnp.sum(lax.all_gather(partial_value, "tok"), axis=0)
     col_ids = lax.broadcasted_iota(jnp.int32, gram_panel.shape, 1)
     row_ids = lax.broadcasted_iota(jnp.int32, gram_panel.shape, 0)
     on_diag = col_ids == blk_index * span_width + row_ids

time: 373 us -> 525 us (1.41)
  waiting for transfers between devices: 332 us -> 471 us
  other arithmetic: 2.53 us -> 15 us
    all_gather x0 -> x1, waiting for transfers between devices: none -> 263 us  [local(): gram_panel = jnp.sum(lax.all_gather(partial_value, 'tok'), axis=0)]
    psum x1 -> x0, waiting for transfers between devices: 107 us -> none  [local(): gram_panel = lax.psum(partial_value, 'tok')]
    all_gather x1, waiting for transfers between devices: 82.6 us -> 66.4 us  [local(): lax.all_gather(w_group, 'blk', axis=1, tiled=True).astype(jnp.float32)]
    reduce_sum x0 -> x1, other arithmetic: none -> 12.5 us  [local(): gram_panel = jnp.sum(lax.all_gather(partial_value, 'tok'), axis=0)]
  transfers between devices with their start and end apart: 4 -> 4, of which waited for: 4 -> 4; matrix products, arithmetic and copies ran while one was open for 3% -> 4% of each run, Pallas kernels for 0% -> 0%
where the time goes in v2:
time: 525 us; the launch traced here: 524 us
  waiting for transfers between devices  471 us (90%)
  other arithmetic  15 us (3%)
  between operations  13.8 us (3%)
  matrix products  12.1 us (2%)
  blocking collectives  6.89 us (1%)
    all_gather x1, waiting for transfers between devices, local(): gram_panel = jnp.sum(lax.all_gather(partial_value, 'tok'), axis=0)  263 us
    all_gather x1, waiting for transfers between devices, local(): lax.all_gather(x_local, 'blk', axis=1, tiled=True)  106 us
    all_gather x1, waiting for transfers between devices, local(): lax.all_gather(w_group, 'blk', axis=1, tiled=True).astype(jnp.float32)  66.4 us
    psum x1, waiting for transfers between devices, local(): denominator, numerator = lax.psum((denominator, numerator), 'mp')  35.2 us
    reduce_sum x1, other arithmetic, local(): gram_panel = jnp.sum(lax.all_gather(partial_value, 'tok'), axis=0)  12.5 us
  transfers between devices with their start and end apart: 4, of which 4 were waited for; matrix products, arithmetic and copies ran while one was open for 4% of the time, Pallas kernels for 0%

profile of v2, /device:TPU:1, one launch (start us, length us, event | category | flops | bytes accessed | tf_op | source)
XLA Modules:
  0.0 524.5 jit_solution(1444759106073881274)
XLA Ops:
  7.2 0.0 copy-start
  7.2 0.0 all-gather.7.cloned.1.call-start
  7.2 0.7 all-gather.7.cloned.1.call-update
  7.9 0.0 all-gather.9.cloned.1.call-start
  8.0 106.5 %all-gather.7.cloned.1.call-done = bf16[1,128,28672]{2,1,0:T(8,128)(2,1)} async-done(((bf16[1,128,896]{2,1,0:T(8,128)(2,1)}), bf16[1,128,28672]{2,1,0:T(8,128)(2,1)}) %all-gather.7.cloned.1.call-update) | async-done | bytes 7340048 | tf_op jit(solution)/shard_map/all_gather | solution.py:24
  114.4 6.0 %fusion = f32[32,28672]{1,0:T(8,128)} fusion(bf16[1,128,28672]{2,1,0:T(8,128)(2,1)} %all-gather.7.cloned.1.call-done, bf16[128,896]{1,0:T(8,128)(2,1)} %bitcast.10), kind=kOutput, calls=%fused_computation | convolution fusion | flops 234881024 | bytes 11042816 | tf_op jit(solution)/shard_map/dot_general | solution.py:22
  120.5 0.0 all-gather.9.cloned.1.call-update
  120.5 0.0 all-gather.11.cloned.1.call-start
  120.5 0.0 copy-done
  120.6 0.7 constant_dynamic-slice_fusion
  121.2 0.0 all-gather.11.cloned.1.call-update
  121.2 0.0 all-reduce.2.cloned.1.call-start
  121.3 262.7 %all-gather.9.cloned.1.call-done = f32[256,28672]{1,0:T(8,128)} async-done(((f32[32,28672]{1,0:T(8,128)}), f32[256,28672]{1,0:T(8,128)}) %all-gather.9.cloned.1.call-update) | async-done | bytes 29360144 | tf_op jit(solution)/shard_map/all_gather | solution.py:28
  384.0 12.5 %reduce_sum.9 = f32[32,28672]{1,0:T(8,128)} reduce(f32[8,32,28672]{2,1,0:T(8,128)} %bitcast.9, f32[]{:T(128)} %constant.7.clone.1), dimensions={0}, to_apply=%region_0.0 | reduce | flops 6422528 | bytes 33030148 | tf_op jit(solution)/shard_map/reduce_sum | solution.py:28
  396.5 2.5 multiply_select_fusion
  399.0 0.0 copy-start.1
  399.0 1.8 copy-done.1
  400.8 0.8 constant_dynamic-slice_fusion.1
  401.6 0.0 all-reduce.2.cloned.1.call-update
  401.6 66.4 %all-gather.11.cloned.1.call-done = bf16[1,64,28672]{2,1,0:T(8,128)(2,1)} async-done(((bf16[1,64,896]{2,1,0:T(8,128)(2,1)}), bf16[1,64,28672]{2,1,0:T(8,128)(2,1)}) %all-gather.11.cloned.1.call-update) | async-done | bytes 3670032 | tf_op jit(solution)/shard_map/all_gather | solution.py:37
  468.0 6.1 %fusion.2 = f32[32,64]{1,0:T(8,128)S(1)} fusion(f32[32,28672]{1,0:T(8,128)} %copy-done.1, bf16[1,64,28672]{2,1,0:T(8,128)(2,1)} %all-gather.11.cloned.1.call-done), kind=kOutput, calls=%fused_computation.3 | convolution fusion | flops 704643072 | bytes 7348224 | tf_op jit(solution)/shard_map/dot_general | solution.py:35
  474.1 6.9 %psum.15 = f32[32,64]{1,0:T(8,128)} all-reduce(f32[32,64]{1,0:T(8,128)S(1)} %fusion.2), channel_id=1, replica_groups=mesh['mp'=2,'blk'=32,'tok'=8] {'mp'}, use_global_device_ids=true, to_apply=%region_2.3 | all-reduce | flops 2048 | bytes 16384 | tf_op jit(solution)/shard_map/psum | solution.py:42
  481.0 35.2 %all-reduce.2.cloned.1.call-done = f32[32,3584]{1,0:T(8,128)} async-done(((f32[32,3584]{1,0:T(8,128)}), f32[32,3584]{1,0:T(8,128)}) %all-reduce.2.cloned.1.call-update) | async-done | bytes 458768 | tf_op jit(solution)/shard_map/psum | solution.py:42
  516.1 1.8 copy.5
  (1 shorter events, 0.0 us)
Async XLA Ops:
  7.2 113.4 %copy-start = (bf16[1,512,896]{2,1,0:T(8,128)(2,1)S(1)}, bf16[1,512,896]{2,1,0:T(8,128)(2,1)}, u32[]{:S(2)}) copy-start(bf16[1,512,896]{2,1,0:T(8,128)(2,1)} %param.3) | copy-start | bytes 2752516
  7.2 107.3 %all-gather.7.cloned.1.call-start = ((), (), s32[]{:S(2)}) async-start(), calls=%async_computation.1 | async-start | bytes 7569408 | tf_op jit(solution)/shard_map/all_gather | solution.py:24
  7.9 376.1 %all-gather.9.cloned.1.call-start = ((), (), s32[]{:S(2)}) async-start(), calls=%async_computation.2 | async-start | bytes 33030144 | tf_op jit(solution)/shard_map/all_gather | solution.py:28
  120.5 347.5 %all-gather.11.cloned.1.call-start = ((), (), s32[]{:S(2)}) async-start(), calls=%async_computation.3 | async-start | bytes 3784704 | tf_op jit(solution)/shard_map/all_gather | solution.py:37
  121.2 394.9 %all-reduce.2.cloned.1.call-start = ((), (), s32[]{:S(2)}) async-start(), calls=%async_computation | async-start | bytes 917504 | tf_op jit(solution)/shard_map/psum | solution.py:42
  399.0 1.8 copy-start.1
Sparse Core Ops, SparseCore 0:
  11.2 103.2 all-gather.6
  120.6 263.3 all-gather.8
  387.2 80.7 all-gather.10
  471.3 44.7 all-reduce.1
